TPU v7x, 32 devices: a whole 2x2x4 slice. The times are simulated.
32 devices in a mesh: gx: 4 (over y, x), gy: 8 (over z, core).
Axes of the slice: x: 2, y: 2, z: 4, core: 2. Of those that a mesh axis runs over, the one named last changes fastest.
Arguments:
- source_heat: float32 [160, 64, 1024], P(None, 'gx', 'gy'), may hold values from -8 to 8
- horiz_coef: float32 [160], replicated, may hold values from 0.5 to 4
- face_coef: float32 [161], replicated, may hold values from 0.25 to 4
- column_inverse: float32 [160, 160], replicated, as said below
Outputs:
- pressure: float32 [160, 64, 1024], P(None, 'gx', 'gy')
- true_residual: float32 [160, 64, 1024], P(None, 'gx', 'gy')
Inputs may be any that keep to these rules, and one draw needn't show every extreme that they name: `column_inverse`: the inverse of the tridiagonal matrix with diagonal 4 horiz_coef[k] + face_coef[k] + face_coef[k+1] and off-diagonal entries -face_coef[k] between levels k-1 and k.
All inputs are finite; a program needn't handle non-finite values.
Results may differ from a plain program's by a relative error of at most 0.0003.
Values sent between devices are 32-bit elements; how exact they have to be, the bound alone decides.
A program may use at most 64 MiB of HBM per device.

v0:
```python
import jax
import jax.numpy as jnp
from jax import lax
from jax.sharding import PartitionSpec as P

ITERS = 3


def with_halo(shard, sides, width):
    for axis, dim in sides:
        size, length = (lax.axis_size(axis), shard.shape[dim])
        up = [(i, (i + 1) % size) for i in range(size)]
        down = [(j, i) for i, j in up]
        last = lax.slice_in_dim(shard, length - width, length, axis=dim)
        leading = lax.slice_in_dim(shard, 0, width, axis=dim)
        before = lax.ppermute(last, axis, up)
        after = lax.ppermute(leading, axis, down)
        shard = jnp.concatenate([before, shard, after], axis=dim)
    return shard


def operate(values_in, horizontal, face_coef):
    padded = with_halo(values_in, (("gx", 1), ("gy", 2)), 1)
    beside = padded[:, 2:, 1:-1] + padded[:, :-2, 1:-1] + padded[:, 1:-1, 2:] + padded[:, 1:-1, :-2]
    zero_layer = jnp.zeros_like(values_in[:1])
    upward = jnp.concatenate([values_in[1:], zero_layer], 0)
    downward = jnp.concatenate([zero_layer, values_in[:-1]], 0)
    lower_face = face_coef[:-1][:, None, None]
    upper_face = face_coef[1:][:, None, None]
    return (
        horizontal[:, None, None] * (4.0 * values_in - beside)
        + upper_face * (values_in - upward)
        + lower_face * (values_in - downward)
    )


def precondition(values_in, column_inverse):
    layout = values_in.shape
    columns = values_in.reshape(layout[0], -1)
    return jnp.dot(column_inverse, columns, precision=lax.Precision.HIGHEST).reshape(layout)


def paired(residual, precond, image):
    return lax.psum((jnp.sum(residual * precond), jnp.sum(precond * image)), ("gx", "gy"))


def on_device(source_heat, horiz_coef, face_coef, column_inverse):
    pressure = jnp.zeros_like(source_heat)
    residual = source_heat
    precond = precondition(residual, column_inverse)
    image = operate(precond, horiz_coef, face_coef)
    inner, product = paired(residual, precond, image)
    step_len = inner / product
    direction, along = (precond, image)
    for iteration in range(ITERS):
        pressure = pressure + step_len * direction
        residual = residual - step_len * along
        if iteration + 1 < ITERS:
            precond = precondition(residual, column_inverse)
            image = operate(precond, horiz_coef, face_coef)
            inner_next, product = paired(residual, precond, image)
            ratio = inner_next / inner
            step_len = inner_next / (product - ratio * inner_next / step_len)
            direction = precond + ratio * direction
            along = image + ratio * along
            inner = inner_next
    true_residual = source_heat - operate(pressure, horiz_coef, face_coef)
    return (pressure, true_residual)


def solution(mesh):
    in_specs = (P(None, "gx", "gy"), P(), P(), P())
    out_specs = (P(None, "gx", "gy"), P(None, "gx", "gy"))
    return jax.shard_map(
        on_device, mesh=mesh, in_specs=in_specs, out_specs=out_specs, check_vma=False
    )
```

profile of v0, /device:TPU:0, one launch (start us, length us, event | category | flops | bytes accessed | tf_op | source)
XLA Modules:
  0.0 253.4 jit_solution(13944040521288698074)
XLA Ops:
  1.6 2.9 %fusion.31 = f32[160,2048]{1,0:T(8,128)S(1)} fusion(f32[160,160]{1,0:T(8,128)S(1)} %copy-done, f32[20,8,16,128]{3,2,1,0:T(8,128)} %bitcast.37), kind=kOutput, calls=%fused_computation.71 | convolution fusion | flops 629145600 | bytes 2723840 | tf_op jit(solution)/shard_map/dot_general | solution.py:40
  7.8 3.0 %collective-permute-start.1 = (f32[160,1,128]{0,2,1:T(8,128)S(1)}, f32[160,1,128]{0,2,1:T(8,128)S(1)}, u32[]{:S(2)}, u32[]{:S(2)}) collective-permute-start(f32[160,1,128]{0,2,1:T(8,128)S(1)} %get-tuple-element.31), channel_id=1, source_target_pairs={{0,8},{8,16},{16,24},{24,0},{1,9},{9,17},{17,25},{25,1},{2,10},{10... | collective-permute-start | bytes 245768 | tf_op jit(solution)/shard_map/ppermute | solution.py:16
  11.8 3.7 %fusion.43 = (f32[159,2048]{1,0:T(8,128)}, f32[159,2048]{1,0:T(8,128)}) fusion(f32[160,2048]{1,0:T(8,128)} %copy-done.8), kind=kLoop, calls=%fused_computation.94 | loop fusion | bytes 5210112 | tf_op jit(solution)/shard_map/slice | solution.py:26
  24.3 2.8 %copy.67 = f32[159,2048]{0,1:T(8,128)} copy(f32[159,2048]{1,0:T(8,128)} %get-tuple-element.39) | data formatting | bytes 2605056 | tf_op jit(solution)/shard_map/slice | solution.py:26
  27.0 2.8 %copy.68 = f32[159,2048]{0,1:T(8,128)} copy(f32[159,2048]{1,0:T(8,128)} %get-tuple-element.40) | data formatting | bytes 2605056 | tf_op jit(solution)/shard_map/slice | solution.py:27
  29.9 5.8 %multiply_reduce_fusion.3 = (f32[]{:T(128)}, f32[160,16,128]{0,2,1:T(8,128)}) fusion(f32[160,16,128]{0,2,1:T(8,128)S(1)} %copy.16, f32[159,16,128]{0,2,1:T(8,128)} %bitcast.42, f32[160]{0:T(256)S(1)} %get-tuple-element.42, f32[159,16,128]{0,2,1:T(8,128)} %bitcast.40, f32[160]{0:T(256)S(1)} %get-tuple-element.41, f32[160,1,128]{0,2,1:T(8,128)S(1)} %collective-permute-done, ...), kind=kLoop, calls=%fused_computation.70 | loop fusion | flops 7208959 | bytes 5415300 | tf_op jit(solution)/shard_map/reduce_sum | solution.py:44
  35.7 38.9 %all-reduce.10 = (f32[]{:T(128)}, f32[]{:T(128)}) all-reduce(f32[]{:T(128)} %multiply_reduce_fusion.4, f32[]{:T(128)} %get-tuple-element.15), channel_id=1, replica_groups=mesh['gx'=4,'gy'=8] {'gx','gy'}, use_global_device_ids=true, to_apply=%region_1.0 | all-reduce | flops 2 | bytes 16 | tf_op jit(solution)/shard_map/psum | solution.py:44
  79.9 3.4 %convolution_bitcast_fusion = f32[160,2048]{1,0:T(8,128)} fusion(f32[160,2048]{0,1:T(8,128)S(1)} %bitcast.32, f32[160,160]{1,0:T(8,128)S(1)} %copy-done), kind=kOutput, calls=%fused_computation | convolution fusion | flops 629145600 | bytes 2723840 | tf_op jit(solution)/shard_map/dot_general | solution.py:40
  88.2 4.0 %collective-permute-done.5 = f32[160,1,128]{0,2,1:T(8,128)S(1)} collective-permute-done((f32[160,1,128]{0,2,1:T(8,128)S(1)}, f32[160,1,128]{0,2,1:T(8,128)S(1)}, u32[]{:S(2)}, u32[]{:S(2)}) %collective-permute-start.5) | collective-permute-done | bytes 81952 | tf_op jit(solution)/shard_map/ppermute | solution.py:16
  98.7 2.8 %copy.70 = f32[159,2048]{0,1:T(8,128)} copy(f32[159,2048]{1,0:T(8,128)} %get-tuple-element.38) | data formatting | bytes 2605056 | tf_op jit(solution)/shard_map/slice | solution.py:27
  101.5 6.4 %multiply_reduce_fusion.1 = (f32[]{:T(128)}, f32[]{:T(128)}, f32[160,16,128]{0,2,1:T(8,128)}) fusion(f32[160,16,128]{0,2,1:T(8,128)S(1)} %bitcast.31, f32[160,16,128]{0,2,1:T(8,128)} %copy-done.3, f32[159,16,128]{0,2,1:T(8,128)} %bitcast.44, f32[160]{0:T(256)S(1)} %get-tuple-element.42, f32[159,16,128]{0,2,1:T(8,128)} %bitcast.43, ...), kind=kLoop, calls=%fused_computation.67 | loop fusion | flops 7864318 | bytes 6726024 | tf_op jit(solution)/shard_map/reduce_sum | solution.py:44
  107.9 40.8 %all-reduce.9 = (f32[]{:T(128)}, f32[]{:T(128)}) all-reduce(f32[]{:T(128)} %get-tuple-element.7, f32[]{:T(128)} %get-tuple-element.6), channel_id=1, replica_groups=mesh['gx'=4,'gy'=8] {'gx','gy'}, use_global_device_ids=true, to_apply=%region_5.0 | all-reduce | flops 2 | bytes 16 | tf_op jit(solution)/shard_map/psum | solution.py:44
  153.1 3.3 %multiply_subtract_fusion = f32[160,16,128]{0,2,1:T(8,128)S(1)} fusion(f32[160,16,128]{0,2,1:T(8,128)} %copy-done.3, f32[160,16,128]{0,2,1:T(8,128)} %get-tuple-element.14, f32[160,16,128]{0,2,1:T(8,128)} %get-tuple-element.16, f32[]{:T(128)S(6)} %div.22, f32[]{:T(128)S(6)} %div.24), kind=kLoop, calls=%fused_computation.66 | loop fusion | flops 1310720 | bytes 5242888 | tf_op jit(solution)/shard_map/sub | solution.py:57
  159.3 2.9 %collective-permute-start.8 = (f32[160,1,128]{2,0,1:T(8,128)S(1)}, f32[160,1,128]{2,0,1:T(8,128)S(1)}, u32[]{:S(2)}, u32[]{:S(2)}) collective-permute-start(f32[160,1,128]{2,0,1:T(8,128)S(1)} %bitcast.48), channel_id=1, source_target_pairs={{8,0},{16,8},{24,16},{0,24},{9,1},{17,9},{25,17},{1,25},{10,2},{18... | collective-permute-start | bytes 245768 | tf_op jit(solution)/shard_map/ppermute | solution.py:17
  164.6 2.8 %collective-permute-done.9 = f32[160,1,128]{2,0,1:T(8,128)S(1)} collective-permute-done((f32[160,1,128]{2,0,1:T(8,128)S(1)}, f32[160,1,128]{2,0,1:T(8,128)S(1)}, u32[]{:S(2)}, u32[]{:S(2)}) %collective-permute-start.9) | collective-permute-done | bytes 81952 | tf_op jit(solution)/shard_map/ppermute | solution.py:16
  167.7 3.5 %collective-permute-start.10 = (f32[160,18,1]{0,1,2:T(8,128)S(1)}, f32[160,18,1]{0,1,2:T(8,128)S(1)}, u32[]{:S(2)}, u32[]{:S(2)}) collective-permute-start(f32[160,18,1]{0,1,2:T(8,128)S(1)} %copy.44), channel_id=1, source_target_pairs={{1,0},{2,1},{3,2},{4,3},{5,4},{6,5},{7,6},{0,7},{9,8},{10,9},{11,1... | collective-permute-start | bytes 34568 | tf_op jit(solution)/shard_map/ppermute | solution.py:17
  173.0 2.8 %copy.71 = f32[159,2048]{0,1:T(8,128)} copy(f32[159,2048]{1,0:T(8,128)} %get-tuple-element.33) | data formatting | bytes 2605056 | tf_op jit(solution)/shard_map/slice | solution.py:26
  178.6 5.4 %fusion.14 = (f32[]{:T(128)}, f32[]{:T(128)}) fusion(f32[160,16,128]{0,2,1:T(8,128)S(1)} %copy.33, f32[160,18,1]{0,2,1:T(1,128)S(1)} %copy.47, f32[160,1,128]{0,2,1:T(8,128)S(1)} %copy.37, f32[160,1,128]{0,2,1:T(8,128)S(1)} %copy.39, f32[160,18,1]{0,2,1:T(1,128)S(1)} %copy.45, f32[159,16,128]{0,2,1:T(8,128)} %bitcast.41, f32[159,16,128]{0,2,1:T(8,128)} %bitcast.39, ...), kind=kLoop, calls=%fused_computation.24 | loop fusion | flops 7864318 | bytes 5415304 | tf_op jit(solution)/shard_map/reduce_sum | solution.py:44
  183.9 37.1 %all-reduce.8 = (f32[]{:T(128)}, f32[]{:T(128)}) all-reduce(f32[]{:T(128)} %get-tuple-element.5, f32[]{:T(128)} %get-tuple-element.4), channel_id=1, replica_groups=mesh['gx'=4,'gy'=8] {'gx','gy'}, use_global_device_ids=true, to_apply=%region_9.0 | all-reduce | flops 2 | bytes 16 | tf_op jit(solution)/shard_map/psum | solution.py:44
  224.9 3.5 %multiply_add_fusion = f32[160,16,128]{0,2,1:T(8,128)S(1)} fusion(f32[160,16,128]{0,2,1:T(8,128)} %copy-done.4, f32[160,16,128]{0,2,1:T(8,128)} %copy-done.1, f32[]{:T(128)S(6)} %div.25, f32[]{:T(128)S(6)} %div.27, f32[]{:T(128)S(6)} %div.22, f32[]{:T(128)S(6)} %div.24, f32[]{:T(128)S(6)} %div.21, f32[160,2048]{0,1:T(8,128)} %copy-done.2), kind=kLoop, calls=%fused_computation.64 | loop fusion | flops 2949120 | bytes 5242900 | tf_op jit(solution)/shard_map/add | solution.py:56
  228.6 2.9 %collective-permute-start.12 = (f32[160,1,128]{2,0,1:T(8,128)S(1)}, f32[160,1,128]{2,0,1:T(8,128)S(1)}, u32[]{:S(2)}, u32[]{:S(2)}) collective-permute-start(f32[160,1,128]{2,0,1:T(8,128)S(1)} %copy.54), channel_id=1, source_target_pairs={{8,0},{16,8},{24,16},{0,24},{9,1},{17,9},{25,17},{1,25},{10,2},{18... | collective-permute-start | bytes 245768 | tf_op jit(solution)/shard_map/ppermute | solution.py:17
  233.8 3.1 %collective-permute-done.13 = f32[160,1,128]{2,0,1:T(8,128)S(1)} collective-permute-done((f32[160,1,128]{2,0,1:T(8,128)S(1)}, f32[160,1,128]{2,0,1:T(8,128)S(1)}, u32[]{:S(2)}, u32[]{:S(2)}) %collective-permute-start.13) | collective-permute-done | bytes 81952 | tf_op jit(solution)/shard_map/ppermute | solution.py:16
  237.2 3.5 %collective-permute-start.14 = (f32[160,18,1]{0,1,2:T(8,128)S(1)}, f32[160,18,1]{0,1,2:T(8,128)S(1)}, u32[]{:S(2)}, u32[]{:S(2)}) collective-permute-start(f32[160,18,1]{0,1,2:T(8,128)S(1)} %copy.60), channel_id=1, source_target_pairs={{1,0},{2,1},{3,2},{4,3},{5,4},{6,5},{7,6},{0,7},{9,8},{10,9},{11,1... | collective-permute-start | bytes 34568 | tf_op jit(solution)/shard_map/ppermute | solution.py:17
  245.2 5.5 %fusion.5 = f32[160,16,128]{0,2,1:T(8,128)} fusion(f32[160,16,128]{0,2,1:T(8,128)} %copy.18, f32[160,18,1]{0,2,1:T(1,128)S(1)} %copy.63, f32[160,1,128]{0,2,1:T(8,128)S(1)} %copy.55, f32[160,16,128]{0,2,1:T(8,128)S(1)} %multiply_add_fusion, f32[160,1,128]{0,2,1:T(8,128)S(1)} %copy.57, f32[160,18,1]{0,2,1:T(1,128)S(1)} %copy.61, ...), kind=kLoop, calls=%fused_computation.7 | loop fusion | flops 6881280 | bytes 6726016 | tf_op jit(solution)/shard_map/sub | solution.py:67
  (93 shorter events, 49.1 us)
Async XLA Ops:
  7.7 22.1 %copy-start.1 = (f32[160,16,128]{0,2,1:T(8,128)}, f32[160,16,128]{0,2,1:T(8,128)S(1)}, u32[]{:S(2)}) copy-start(f32[160,16,128]{0,2,1:T(8,128)S(1)} %copy.16) | copy-start | bytes 3932164
  7.8 8.3 %collective-permute-start.1 = (f32[160,1,128]{0,2,1:T(8,128)S(1)}, f32[160,1,128]{0,2,1:T(8,128)S(1)}, u32[]{:S(2)}, u32[]{:S(2)}) collective-permute-start(f32[160,1,128]{0,2,1:T(8,128)S(1)} %get-tuple-element.31), channel_id=1, source_target_pairs={{0,8},{8,16},{16,24},{24,0},{1,9},{9,17},{17,25},{25,1},{2,10},{10... | collective-permute-start | bytes 245768 | tf_op jit(solution)/shard_map/ppermute | solution.py:16
  10.8 4.7 %copy-start.14 = (f32[161]{0:T(256)S(1)}, f32[161]{0:T(256)}, u32[]{:S(2)}) copy-start(f32[161]{0:T(256)} %param.6) | copy-start | bytes 1936
  10.8 7.5 %collective-permute-start = (f32[160,1,128]{0,2,1:T(8,128)S(1)}, f32[160,1,128]{0,2,1:T(8,128)S(1)}, u32[]{:S(2)}, u32[]{:S(2)}) collective-permute-start(f32[160,1,128]{0,2,1:T(8,128)S(1)} %get-tuple-element.32), channel_id=1, source_target_pairs={{8,0},{16,8},{24,16},{0,24},{9,1},{17,9},{25,17},{1,25},{10,2},{18... | collective-permute-start | bytes 245768 | tf_op jit(solution)/shard_map/ppermute | solution.py:17
  11.8 8.7 %copy-start.11 = (f32[20,8,16,128]{3,2,1,0:T(8,128)S(1)}, f32[20,8,16,128]{3,2,1,0:T(8,128)}, u32[]{:S(2)}) copy-start(f32[20,8,16,128]{3,2,1,0:T(8,128)} %copy.77) | copy-start | bytes 3932164
  15.5 5.1 %copy-start.10 = (f32[160,16,128]{2,1,0:T(8,128)S(1)}, f32[160,16,128]{2,1,0:T(8,128)}, u32[]{:S(2)}) copy-start(f32[160,16,128]{2,1,0:T(8,128)} %param.4) | copy-start | bytes 3932164
  18.3 11.5 %collective-permute-start.2 = (f32[160,18,1]{0,2,1:T(1,128)S(1)}, f32[160,18,1]{0,2,1:T(1,128)S(1)}, u32[]{:S(2)}, u32[]{:S(2)}) collective-permute-start(f32[160,18,1]{0,2,1:T(1,128)S(1)} %get-tuple-element.23), channel_id=1, source_target_pairs={{1,0},{2,1},{3,2},{4,3},{5,4},{6,5},{7,6},{0,7},{9,8},{10,9},{11,1... | collective-permute-start | bytes 34568 | tf_op jit(solution)/shard_map/ppermute | solution.py:17
  20.6 9.3 %collective-permute-start.3 = (f32[160,18,1]{0,2,1:T(1,128)S(1)}, f32[160,18,1]{0,2,1:T(1,128)S(1)}, u32[]{:S(2)}, u32[]{:S(2)}) collective-permute-start(f32[160,18,1]{0,2,1:T(1,128)S(1)} %get-tuple-element.24), channel_id=1, source_target_pairs={{0,1},{1,2},{2,3},{3,4},{4,5},{5,6},{6,7},{7,0},{8,9},{9,10},{10,1... | collective-permute-start | bytes 34568 | tf_op jit(solution)/shard_map/ppermute | solution.py:16
  85.2 16.3 %copy-start.2 = (f32[160,2048]{0,1:T(8,128)}, f32[160,2048]{0,1:T(8,128)S(1)}, u32[]{:S(2)}) copy-start(f32[160,2048]{0,1:T(8,128)S(1)} %copy.73) | copy-start | bytes 3932164
  85.2 9.1 %copy-start.7 = (f32[160,2048]{1,0:T(8,128)S(1)}, f32[160,2048]{1,0:T(8,128)}, u32[]{:S(2)}) copy-start(f32[160,2048]{1,0:T(8,128)} %convolution_bitcast_fusion) | copy-start | bytes 3932164
  85.2 7.0 %collective-permute-start.5 = (f32[160,1,128]{0,2,1:T(8,128)S(1)}, f32[160,1,128]{0,2,1:T(8,128)S(1)}, u32[]{:S(2)}, u32[]{:S(2)}) collective-permute-start(f32[160,1,128]{0,2,1:T(8,128)S(1)} %get-tuple-element.29), channel_id=1, source_target_pairs={{0,8},{8,16},{16,24},{24,0},{1,9},{9,17},{17,25},{25,1},{2,10},{10... | collective-permute-start | bytes 245768 | tf_op jit(solution)/shard_map/ppermute | solution.py:16
  87.5 6.1 %collective-permute-start.4 = (f32[160,1,128]{0,2,1:T(8,128)S(1)}, f32[160,1,128]{0,2,1:T(8,128)S(1)}, u32[]{:S(2)}, u32[]{:S(2)}) collective-permute-start(f32[160,1,128]{0,2,1:T(8,128)S(1)} %get-tuple-element.30), channel_id=1, source_target_pairs={{8,0},{16,8},{24,16},{0,24},{9,1},{17,9},{25,17},{1,25},{10,2},{18... | collective-permute-start | bytes 245768 | tf_op jit(solution)/shard_map/ppermute | solution.py:17
  93.7 7.8 %collective-permute-start.6 = (f32[160,18,1]{0,2,1:T(1,128)S(1)}, f32[160,18,1]{0,2,1:T(1,128)S(1)}, u32[]{:S(2)}, u32[]{:S(2)}) collective-permute-start(f32[160,18,1]{0,2,1:T(1,128)S(1)} %get-tuple-element.21), channel_id=1, source_target_pairs={{1,0},{2,1},{3,2},{4,3},{5,4},{6,5},{7,6},{0,7},{9,8},{10,9},{11,1... | collective-permute-start | bytes 34568 | tf_op jit(solution)/shard_map/ppermute | solution.py:17
  93.8 7.7 %collective-permute-start.7 = (f32[160,18,1]{0,2,1:T(1,128)S(1)}, f32[160,18,1]{0,2,1:T(1,128)S(1)}, u32[]{:S(2)}, u32[]{:S(2)}) collective-permute-start(f32[160,18,1]{0,2,1:T(1,128)S(1)} %get-tuple-element.22), channel_id=1, source_target_pairs={{0,1},{1,2},{2,3},{3,4},{4,5},{5,6},{6,7},{7,0},{8,9},{9,10},{10,1... | collective-permute-start | bytes 34568 | tf_op jit(solution)/shard_map/ppermute | solution.py:16
  159.3 5.3 %collective-permute-start.8 = (f32[160,1,128]{2,0,1:T(8,128)S(1)}, f32[160,1,128]{2,0,1:T(8,128)S(1)}, u32[]{:S(2)}, u32[]{:S(2)}) collective-permute-start(f32[160,1,128]{2,0,1:T(8,128)S(1)} %bitcast.48), channel_id=1, source_target_pairs={{8,0},{16,8},{24,16},{0,24},{9,1},{17,9},{25,17},{1,25},{10,2},{18... | collective-permute-start | bytes 245768 | tf_op jit(solution)/shard_map/ppermute | solution.py:17
  162.1 5.3 %collective-permute-start.9 = (f32[160,1,128]{2,0,1:T(8,128)S(1)}, f32[160,1,128]{2,0,1:T(8,128)S(1)}, u32[]{:S(2)}, u32[]{:S(2)}) collective-permute-start(f32[160,1,128]{2,0,1:T(8,128)S(1)} %bitcast.47), channel_id=1, source_target_pairs={{0,8},{8,16},{16,24},{24,0},{1,9},{9,17},{17,25},{25,1},{2,10},{10... | collective-permute-start | bytes 245768 | tf_op jit(solution)/shard_map/ppermute | solution.py:16
  164.4 14.1 %copy-start.4 = (f32[160,16,128]{0,2,1:T(8,128)}, f32[160,16,128]{0,2,1:T(8,128)S(1)}, u32[]{:S(2)}) copy-start(f32[160,16,128]{0,2,1:T(8,128)S(1)} %copy.33) | copy-start | bytes 3932164
  167.6 3.7 %copy-start.6 = (f32[2048,160]{0,1:T(8,128)S(1)}, f32[2048,160]{0,1:T(8,128)}, u32[]{:S(2)}) copy-start(f32[2048,160]{0,1:T(8,128)} %copy-done.5) | copy-start | bytes 3932164
  167.6 10.9 %collective-permute-start.11 = (f32[160,18,1]{0,1,2:T(8,128)S(1)}, f32[160,18,1]{0,1,2:T(8,128)S(1)}, u32[]{:S(2)}, u32[]{:S(2)}) collective-permute-start(f32[160,18,1]{0,1,2:T(8,128)S(1)} %copy.46), channel_id=1, source_target_pairs={{0,1},{1,2},{2,3},{3,4},{4,5},{5,6},{6,7},{7,0},{8,9},{9,10},{10,1... | collective-permute-start | bytes 34568 | tf_op jit(solution)/shard_map/ppermute | solution.py:16
  167.7 10.8 %collective-permute-start.10 = (f32[160,18,1]{0,1,2:T(8,128)S(1)}, f32[160,18,1]{0,1,2:T(8,128)S(1)}, u32[]{:S(2)}, u32[]{:S(2)}) collective-permute-start(f32[160,18,1]{0,1,2:T(8,128)S(1)} %copy.44), channel_id=1, source_target_pairs={{1,0},{2,1},{3,2},{4,3},{5,4},{6,5},{7,6},{0,7},{9,8},{10,9},{11,1... | collective-permute-start | bytes 34568 | tf_op jit(solution)/shard_map/ppermute | solution.py:17
  228.6 5.1 %collective-permute-start.12 = (f32[160,1,128]{2,0,1:T(8,128)S(1)}, f32[160,1,128]{2,0,1:T(8,128)S(1)}, u32[]{:S(2)}, u32[]{:S(2)}) collective-permute-start(f32[160,1,128]{2,0,1:T(8,128)S(1)} %copy.54), channel_id=1, source_target_pairs={{8,0},{16,8},{24,16},{0,24},{9,1},{17,9},{25,17},{1,25},{10,2},{18... | collective-permute-start | bytes 245768 | tf_op jit(solution)/shard_map/ppermute | solution.py:17
  231.5 5.4 %collective-permute-start.13 = (f32[160,1,128]{2,0,1:T(8,128)S(1)}, f32[160,1,128]{2,0,1:T(8,128)S(1)}, u32[]{:S(2)}, u32[]{:S(2)}) collective-permute-start(f32[160,1,128]{2,0,1:T(8,128)S(1)} %copy.56), channel_id=1, source_target_pairs={{0,8},{8,16},{16,24},{24,0},{1,9},{9,17},{17,25},{25,1},{2,10},{10... | collective-permute-start | bytes 245768 | tf_op jit(solution)/shard_map/ppermute | solution.py:16
  237.1 8.0 %collective-permute-start.15 = (f32[160,18,1]{0,1,2:T(8,128)S(1)}, f32[160,18,1]{0,1,2:T(8,128)S(1)}, u32[]{:S(2)}, u32[]{:S(2)}) collective-permute-start(f32[160,18,1]{0,1,2:T(8,128)S(1)} %copy.62), channel_id=1, source_target_pairs={{0,1},{1,2},{2,3},{3,4},{4,5},{5,6},{6,7},{7,0},{8,9},{9,10},{10,1... | collective-permute-start | bytes 34568 | tf_op jit(solution)/shard_map/ppermute | solution.py:16
  237.2 8.0 %collective-permute-start.14 = (f32[160,18,1]{0,1,2:T(8,128)S(1)}, f32[160,18,1]{0,1,2:T(8,128)S(1)}, u32[]{:S(2)}, u32[]{:S(2)}) collective-permute-start(f32[160,18,1]{0,1,2:T(8,128)S(1)} %copy.60), channel_id=1, source_target_pairs={{1,0},{2,1},{3,2},{4,3},{5,4},{6,5},{7,6},{0,7},{9,8},{10,9},{11,1... | collective-permute-start | bytes 34568 | tf_op jit(solution)/shard_map/ppermute | solution.py:17
  (7 other events, 15.6 us)
where the time goes:
time: 254 us; the launch traced here: 253 us
  blocking collectives  117 us (46%)
  local copies, waits for them, and re-layouts  44 us (17%)
  other arithmetic  33.5 us (13%)
  starting transfers between devices  23.3 us (9%)
  waiting for transfers between devices  16.4 us (6%)
  between operations  10.8 us (4%)
  matrix products  8.72 us (3%)
    psum x3, blocking collectives, paired(): lax.psum((jnp.sum(residual * precond), jnp.sum(precond * image)), ('gx',...  117 us
    slice x7, local copies, waits for them, and re-layouts, operate(): upward = jnp.concatenate([values_in[1:], zero_layer], 0)  18.1 us
    reduce_sum x3, other arithmetic, paired(): jnp.sum(precond * image)  17.5 us
    ppermute x8, starting transfers between devices, with_halo(): after = lax.ppermute(leading, axis, down)  16.8 us
    unnamed x35, local copies, waits for them, and re-layouts  11.2 us
    ppermute x8, waiting for transfers between devices, with_halo(): before = lax.ppermute(last, axis, up)  10.5 us
    dot_general x3, matrix products, precondition(): jnp.dot(column_inverse, columns, precision=lax.Precision.HIGHEST)  8.72 us
    slice x3, local copies, waits for them, and re-layouts, operate(): downward = jnp.concatenate([zero_layer, values_in[:-1]], 0)  8.36 us
  transfers between devices with their start and end apart: 16, of which 8 were waited for; matrix products, arithmetic and copies ran while one was open for 13% of the time, Pallas kernels for 0%

commit v1 on v0

v1 whole, which is shorter than its diff:
```python
import functools

import jax
import jax.numpy as jnp
from jax import lax
from jax.experimental import pallas as pl
from jax.experimental.pallas import tpu as pltpu
from jax.sharding import PartitionSpec as P

ITERS = 3
MESH = pl.DeviceIdType.MESH
F32 = jnp.float32
BF16 = jnp.bfloat16


def split2(v):
    high = v.astype(BF16)
    low = (v - high.astype(F32)).astype(BF16)
    return high, low


def folded(v):
    return jnp.sum(v.reshape(v.shape[0] // 8, 8, v.shape[1]), axis=0)


def coefficients(m):
    rho, delta, press = [None], [None], []
    inner = m[0]
    one = jnp.ones_like(m[0])
    rho, delta = [one], [one]
    for it in range(ITERS):
        n = len(delta)
        dad = 0.0
        for i in range(n):
            for j in range(n):
                dad = dad + delta[i] * delta[j] * (m[i + j] - m[i + j + 1])
        step = inner / dad
        press = [
            (press[i] if i < len(press) else 0.0) + step * delta[i] for i in range(n)
        ]
        image = [
            (delta[i] if i < n else 0.0) - (delta[i - 1] if i else 0.0)
            for i in range(n + 1)
        ]
        rho = [(rho[i] if i < n else 0.0) - step * image[i] for i in range(n + 1)]
        if it + 1 < ITERS:
            inner_next = 0.0
            for i in range(n + 1):
                for j in range(n + 1):
                    inner_next = inner_next + rho[i] * rho[j] * m[i + j]
            ratio = inner_next / inner
            delta = [
                rho[i] + (ratio * delta[i] if i < n else 0.0) for i in range(n + 1)
            ]
            inner = inner_next
    resid = [
        (press[i] if i < ITERS else 0.0) for i in range(ITERS)
    ]
    resid = (
        [1.0 - press[0]]
        + [press[i - 1] - press[i] for i in range(1, ITERS)]
        + [press[ITERS - 1]]
    )
    return press, resid


def kernel(
    sx, sy, b_hbm, h_ref, m_ref, p_hbm, r_hbm,
    bs, ws, mcat, pack, halo, part, slots_x, mid, slots_y,
    load_sem, store_sem, xs_sem, xr_sem, ys_sem, yr_sem,
    ax_s, ax_r, ay_s, ay_r,
):
    K, X, Y = b_hbm.shape
    G = Y // (2 * X)
    KG = K // G
    ix, iy = lax.axis_index("gx"), lax.axis_index("gy")
    xn, xp = lax.rem(ix + 1, sx), lax.rem(ix + sx - 1, sx)
    yn, yp = lax.rem(iy + 1, sy), lax.rem(iy + sy - 1, sy)

    barrier = pltpu.get_barrier_semaphore()
    for d in range(1, sx):
        pl.semaphore_signal(
            barrier, inc=1, device_id={"gx": lax.rem(ix + d, sx)}, device_id_type=MESH
        )
    for d in range(1, sy):
        pl.semaphore_signal(
            barrier, inc=1, device_id={"gy": lax.rem(iy + d, sy)}, device_id_type=MESH
        )

    order = [0, X - 1] + list(range(1, X - 1))
    loads = {
        x: pltpu.make_async_copy(b_hbm.at[:, x, :], bs.at[0, x], load_sem.at[x])
        for x in order
    }
    for x in order:
        loads[x].start()

    m1, m2 = split2(m_ref[...])
    mcat[...] = jnp.concatenate([m1.astype(F32), m1.astype(F32), m2.astype(F32)], axis=1).astype(BF16)
    rows = lax.broadcasted_iota(jnp.int32, (K, K), 0)
    cols = lax.broadcasted_iota(jnp.int32, (K, K), 1)
    h_col = jnp.sum(jnp.where(rows == cols, h_ref[...], 0.0), axis=1, keepdims=True)
    h_b = jnp.broadcast_to(h_col, (K, Y))
    lane = lax.broadcasted_iota(jnp.int32, (KG, Y), 1)
    lane_full = lax.broadcasted_iota(jnp.int32, (K, Y), 1)

    def matmul(v0, v1):
        h0, l0 = split2(v0)
        h1, l1 = split2(v1)
        high = jnp.concatenate([h0, h1], axis=1)
        low = jnp.concatenate([l0, l1], axis=1)
        stacked = jnp.concatenate([high, low, high], axis=0)
        out = jnp.dot(mcat[...], stacked, preferred_element_type=F32)
        return out[:, :Y], out[:, Y:]

    def packed(j, x, v):
        acc = pack[j]
        for g in range(G):
            shift = lax.rem(2 * X * g + 2 * x, Y)
            turned = pltpu.roll(v[g * KG:(g + 1) * KG], shift, 1)
            here = (lane == shift) | (lane == lax.rem(shift + Y - 1, Y))
            acc = jnp.where(here, turned, acc)
        pack[j] = acc

    def beside(j, x):
        v = ws[j, x + 1]
        c = halo[j]
        turned = jnp.concatenate(
            [
                pltpu.roll(c, lax.rem(2 * Y - 2 * X * g - 2 * x, Y), 1)
                for g in range(G)
            ],
            axis=0,
        )
        left = jnp.where(lane_full == 0, turned, pltpu.roll(v, 1, 1))
        right = jnp.where(lane_full == Y - 1, turned, pltpu.roll(v, Y - 1, 1))
        total = ws[j, x] + ws[j, x + 2] + left + right
        return v, total

    def through_m(j, x0, x1, v0, v1):
        w0, w1 = matmul(v0, v1)
        ws[j, x0 + 1] = w0
        ws[j, x1 + 1] = w1
        packed(j, x0, w0)
        packed(j, x1, w1)
        return folded(v0 * w0 + v1 * w1)

    def level(j, x0, x1):
        w0, s0 = beside(j, x0)
        w1, s1 = beside(j, x1)
        b0, b1 = h_b * s0, h_b * s1
        bs[j + 1, x0] = b0
        bs[j + 1, x1] = b1
        odd = folded(b0 * w0 + b1 * w1)
        even = None
        if j + 1 < ITERS:
            even = through_m(j + 1, x0, x1, b0, b1)
        return odd, even

    def x_copies(j):
        return (
            pltpu.make_async_remote_copy(
                src_ref=ws.at[j, X], dst_ref=ws.at[j, 0],
                send_sem=xs_sem.at[j, 0], recv_sem=xr_sem.at[j, 0],
                device_id={"gx": xn}, device_id_type=MESH,
            ),
            pltpu.make_async_remote_copy(
                src_ref=ws.at[j, 1], dst_ref=ws.at[j, X + 1],
                send_sem=xs_sem.at[j, 1], recv_sem=xr_sem.at[j, 1],
                device_id={"gx": xp}, device_id_type=MESH,
            ),
        )

    def y_copies(j):
        return (
            pltpu.make_async_remote_copy(
                src_ref=pack.at[j], dst_ref=pack.at[ITERS + j],
                send_sem=ys_sem.at[j, 0], recv_sem=yr_sem.at[j, 0],
                device_id={"gy": yn}, device_id_type=MESH,
            ),
            pltpu.make_async_remote_copy(
                src_ref=pack.at[j], dst_ref=pack.at[2 * ITERS + j],
                send_sem=ys_sem.at[j, 1], recv_sem=yr_sem.at[j, 1],
                device_id={"gy": yp}, device_id_type=MESH,
            ),
        )

    zero = jnp.zeros((8, Y), F32)
    moments = [zero] * (2 * ITERS)
    for j in range(ITERS):
        pack[j] = jnp.zeros((KG, Y), F32)

    loads[0].wait()
    loads[X - 1].wait()
    even = through_m(0, 0, X - 1, bs[0, 0], bs[0, X - 1])
    pl.semaphore_wait(barrier, sx - 1 + sy - 1)
    sent_x = [x_copies(0)]
    for copy in sent_x[0]:
        copy.start()
    for x in range(1, X - 1):
        loads[x].wait()

    def first(i, acc):
        x0 = 2 * i + 1
        return acc + through_m(0, x0, x0 + 1, bs[0, x0], bs[0, x0 + 1])

    moments[0] = lax.fori_loop(0, (X - 2) // 2, first, even)
    sent_y = [y_copies(0)]
    for copy in sent_y[0]:
        copy.start()

    for j in range(ITERS):
        for copy in sent_y[j]:
            copy.wait()
        from_left, from_right = pack[ITERS + j], pack[2 * ITERS + j]
        halo[j] = jnp.where(
            lane % 2 == 0, pltpu.roll(from_left, 1, 1), pltpu.roll(from_right, Y - 1, 1)
        )

        def inside(i, acc):
            x0 = 2 * i + 1
            odd, even = level(j, x0, x0 + 1)
            if even is None:
                return (acc[0] + odd,)
            return (acc[0] + odd, acc[1] + even)

        start = (zero,) if j + 1 == ITERS else (zero, zero)
        got = lax.fori_loop(0, (X - 2) // 2, inside, start)
        for copy in sent_x[j]:
            copy.wait()
        odd, even = level(j, 0, X - 1)
        moments[2 * j + 1] = got[0] + odd
        if j + 1 < ITERS:
            moments[2 * j + 2] = got[1] + even
            sent_x.append(x_copies(j + 1))
            for copy in sent_x[j + 1]:
                copy.start()
            sent_y.append(y_copies(j + 1))
            for copy in sent_y[j + 1]:
                copy.start()

    part[...] = jnp.concatenate(
        [jnp.sum(t, axis=0, keepdims=True) for t in moments]
        + [jnp.zeros((8 - 2 * ITERS, Y), F32)],
        axis=0,
    )

    def total_over(axis, me, size, source, slots, send_sem, recv_sem):
        copies = []
        for d in range(1, size):
            copies.append(
                pltpu.make_async_remote_copy(
                    src_ref=source, dst_ref=slots.at[d - 1],
                    send_sem=send_sem.at[d - 1], recv_sem=recv_sem.at[d - 1],
                    device_id={axis: lax.rem(me + d, size)}, device_id_type=MESH,
                )
            )
            copies[-1].start()
        total = source[...]
        for d in range(1, size):
            copies[d - 1].wait()
            total = total + slots[d - 1]
        return total

    mid[...] = total_over("gx", ix, sx, part, slots_x, ax_s, ax_r)
    total = total_over("gy", iy, sy, mid, slots_y, ay_s, ay_r)
    summed = jnp.broadcast_to(jnp.sum(total, axis=1, keepdims=True), (8, Y))
    press, resid = coefficients([summed[i:i + 1] for i in range(2 * ITERS)])

    for x in range(X):
        p = press[0] * ws[0, x + 1]
        r = resid[0] * bs[0, x]
        for j in range(1, ITERS):
            p = p + press[j] * ws[j, x + 1]
        for j in range(1, ITERS + 1):
            r = r + resid[j] * bs[j, x]
        ws[0, x + 1] = p
        bs[0, x] = r
        pltpu.make_async_copy(ws.at[0, x + 1], p_hbm.at[:, x, :], store_sem.at[0, x]).start()
        pltpu.make_async_copy(bs.at[0, x], r_hbm.at[:, x, :], store_sem.at[1, x]).start()
    for x in range(X):
        pltpu.make_async_copy(ws.at[0, x + 1], p_hbm.at[:, x, :], store_sem.at[0, x]).wait()
        pltpu.make_async_copy(bs.at[0, x], r_hbm.at[:, x, :], store_sem.at[1, x]).wait()


def on_device(sx, sy, source_heat, horiz_coef, face_coef, column_inverse):
    K, X, Y = source_heat.shape
    KG = K // (Y // (2 * X))
    any_spec = pl.BlockSpec(memory_space=pl.ANY)
    vmem = pl.BlockSpec(memory_space=pltpu.VMEM)
    dma = pltpu.SemaphoreType.DMA
    out = jax.ShapeDtypeStruct((K, X, Y), F32)
    return pl.pallas_call(
        functools.partial(kernel, sx, sy),
        out_shape=(out, out),
        in_specs=[any_spec, vmem, vmem],
        out_specs=(any_spec, any_spec),
        scratch_shapes=[
            pltpu.VMEM((ITERS + 1, X, K, Y), F32),
            pltpu.VMEM((ITERS, X + 2, K, Y), F32),
            pltpu.VMEM((K, 3 * K), BF16),
            pltpu.VMEM((3 * ITERS, KG, Y), F32),
            pltpu.VMEM((ITERS, KG, Y), F32),
            pltpu.VMEM((8, Y), F32),
            pltpu.VMEM((sx - 1, 8, Y), F32),
            pltpu.VMEM((8, Y), F32),
            pltpu.VMEM((sy - 1, 8, Y), F32),
            dma((X,)),
            dma((2, X)),
            dma((ITERS, 2)),
            dma((ITERS, 2)),
            dma((ITERS, 2)),
            dma((ITERS, 2)),
            dma((sx - 1,)),
            dma((sx - 1,)),
            dma((sy - 1,)),
            dma((sy - 1,)),
        ],
        compiler_params=pltpu.CompilerParams(
            collective_id=0, has_side_effects=True, vmem_limit_bytes=40 << 20
        ),
        name="pcg",
    )(source_heat, horiz_coef.reshape(1, K), column_inverse)


def solution(mesh):
    in_specs = (P(None, "gx", "gy"), P(), P(), P())
    out_specs = (P(None, "gx", "gy"), P(None, "gx", "gy"))
    body = functools.partial(on_device, mesh.shape["gx"], mesh.shape["gy"])
    return jax.shard_map(
        body, mesh=mesh, in_specs=in_specs, out_specs=out_specs, check_vma=False
    )
```

time: 254 us -> 41.7 us (0.16)
  blocking collectives: 117 us -> 0 us
  local copies, waits for them, and re-layouts: 44 us -> 5.02 us
  Pallas kernels: 0 us -> 35.8 us
  other arithmetic: 33.5 us -> 0 us
  starting transfers between devices: 23.3 us -> 0 us
  waiting for transfers between devices: 16.4 us -> 0 us
  between operations: 10.8 us -> 0.65 us
  matrix products: 8.72 us -> 0 us
    psum x3 -> x0, blocking collectives: 117 us -> none  [paired(): lax.psum((jnp.sum(residual * precond), jnp.sum(precond * image)), ('gx',...]
    pallas_call x0 -> x1, Pallas kernels: none -> 35.8 us  [on_device(): pl.pallas_call(functools.partial(kernel, sx, sy), out_shape=(out, out), i...]
    slice x21 -> x0, local copies, waits for them, and re-layouts: 26.9 us -> none  [the longest x7 18.1 us: operate(): upward = jnp.concatenate([values_in[1:], zero_layer], 0)]
    ppermute x16 -> x0, starting transfers between devices: 23.3 us -> none  [the longest x8 16.8 us: with_halo(): after = lax.ppermute(leading, axis, down)]
    reduce_sum x4 -> x0, other arithmetic: 18.5 us -> none  [the longest x3 17.5 us: paired(): jnp.sum(precond * image)]
    ppermute x16 -> x0, waiting for transfers between devices: 16.4 us -> none  [the longest x8 10.5 us: with_halo(): before = lax.ppermute(last, axis, up)]
    sub x3 -> x0, other arithmetic: 11.4 us -> none  [the longest x2 5.91 us: on_device(): residual = residual - step_len * along]
    dot_general x3 -> x0, matrix products: 8.72 us -> none  [precondition(): jnp.dot(column_inverse, columns, precision=lax.Precision.HIGHEST)]
  transfers between devices with their start and end apart: 16 -> 0, of which waited for: 8 -> 0; matrix products, arithmetic and copies ran while one was open for 13% -> 0% of each run, Pallas kernels for 0% -> 0%
where the time goes in v1:
time: 41.7 us; the launch traced here: 41.5 us
  Pallas kernels  35.8 us (86%)
  local copies, waits for them, and re-layouts  5.02 us (12%)
  between operations  0.65 us (2%)
    pallas_call x1, Pallas kernels, on_device(): pl.pallas_call(functools.partial(kernel, sx, sy), out_shape=(out, out), i...  35.8 us
    unnamed x8, local copies, waits for them, and re-layouts  5.02 us

profile of v1, /device:TPU:0, one launch (start us, length us, event | category | flops | bytes accessed | tf_op | source)
XLA Modules:
  0.0 41.5 jit_solution(1386737545963679042)
XLA Ops:
  0.6 0.0 copy-start
  0.6 1.3 %copy-done = f32[160,16,128]{2,1,0:T(8,128)S(1)} copy-done((f32[160,16,128]{2,1,0:T(8,128)S(1)}, f32[160,16,128]{2,1,0:T(8,128)}, u32[]{:S(2)}) %copy-start) | copy-done | bytes 1310744
  1.9 0.0 copy-start.1
  1.9 0.9 %copy-done.1 = f32[160,160]{1,0:T(8,128)S(1)} copy-done((f32[160,160]{1,0:T(8,128)S(1)}, f32[160,160]{1,0:T(8,128)}, u32[]{:S(2)}) %copy-start.1) | copy-done | bytes 102424
  2.9 0.0 copy-start.2
  2.9 0.7 %copy-done.2 = f32[160]{0:T(256)S(1)} copy-done((f32[160]{0:T(256)S(1)}, f32[160]{0:T(256)}, u32[]{:S(2)}) %copy-start.2) | copy-done | bytes 664
  3.5 35.8 %pcg.1 = (f32[160,16,128]{2,1,0:T(8,128)S(1)}, f32[160,16,128]{2,1,0:T(8,128)S(1)}) custom-call(f32[160,16,128]{2,1,0:T(8,128)S(1)} %copy-done, f32[1,160]{1,0:T(1,128)S(1)} %bitcast.1, f32[160,160]{1,0:T(8,128)S(1)} %copy-done.1), custom_call_target="tpu_custom_call" | custom-call | tf_op jit(solution)/shard_map/pcg/pallas_call | solution.py:293
  39.4 1.1 %copy.7 = f32[160,16,128]{2,1,0:T(8,128)} copy(f32[160,16,128]{2,1,0:T(8,128)S(1)} %get-tuple-element.4) | data formatting | bytes 2621440
  40.4 1.1 %copy.8 = f32[160,16,128]{2,1,0:T(8,128)} copy(f32[160,16,128]{2,1,0:T(8,128)S(1)} %get-tuple-element.5) | data formatting | bytes 2621440
Async XLA Ops:
  0.6 1.3 %copy-start = (f32[160,16,128]{2,1,0:T(8,128)S(1)}, f32[160,16,128]{2,1,0:T(8,128)}, u32[]{:S(2)}) copy-start(f32[160,16,128]{2,1,0:T(8,128)} %b_hbm.1) | copy-start | bytes 3932164
  1.9 0.9 %copy-start.1 = (f32[160,160]{1,0:T(8,128)S(1)}, f32[160,160]{1,0:T(8,128)}, u32[]{:S(2)}) copy-start(f32[160,160]{1,0:T(8,128)} %m_ref.1) | copy-start | bytes 307204
  2.9 0.7 %copy-start.2 = (f32[160]{0:T(256)S(1)}, f32[160]{0:T(256)}, u32[]{:S(2)}) copy-start(f32[160]{0:T(256)} %param.5) | copy-start | bytes 1924

commit v2 on v1

--- a/solution.py
+++ b/solution.py
@@ -24,7 +24,7 @@
 
 
 def coefficients(m):
-    rho, delta, press = [None], [None], []
+    press = []
     inner = m[0]
     one = jnp.ones_like(m[0])
     rho, delta = [one], [one]
@@ -53,9 +53,6 @@
                 rho[i] + (ratio * delta[i] if i < n else 0.0) for i in range(n + 1)
             ]
             inner = inner_next
-    resid = [
-        (press[i] if i < ITERS else 0.0) for i in range(ITERS)
-    ]
     resid = (
         [1.0 - press[0]]
         + [press[i - 1] - press[i] for i in range(1, ITERS)]
@@ -65,9 +62,9 @@
 
 
 def kernel(
-    sx, sy, b_hbm, h_ref, m_ref, p_hbm, r_hbm,
-    bs, ws, mcat, pack, halo, part, slots_x, mid, slots_y,
-    load_sem, store_sem, xs_sem, xr_sem, ys_sem, yr_sem,
+    sx, sy, b_hbm, h_hbm, m_hbm, bs, ws, coef,
+    h_ref, m_ref, mcat, pack, halo, part, slots_x, mid, slots_y,
+    load_sem, small_sem, xs_sem, xr_sem, ys_sem, yr_sem,
     ax_s, ax_r, ay_s, ay_r,
 ):
     K, X, Y = b_hbm.shape
@@ -92,8 +89,14 @@
         x: pltpu.make_async_copy(b_hbm.at[:, x, :], bs.at[0, x], load_sem.at[x])
         for x in order
     }
+    load_h = pltpu.make_async_copy(h_hbm, h_ref, small_sem.at[0])
+    load_m = pltpu.make_async_copy(m_hbm, m_ref, small_sem.at[1])
+    load_m.start()
+    load_h.start()
     for x in order:
         loads[x].start()
+    load_m.wait()
+    load_h.wait()
 
     m1, m2 = split2(m_ref[...])
     mcat[...] = jnp.concatenate([m1.astype(F32), m1.astype(F32), m2.astype(F32)], axis=1).astype(BF16)
@@ -122,8 +125,15 @@
             acc = jnp.where(here, turned, acc)
         pack[j] = acc
 
+    def turned_sum(v):
+        return pltpu.roll(v, 1, 1) + pltpu.roll(v, Y - 1, 1)
+
+    def periodic(j, x):
+        bs[j + 1, x] = ws[j, x] + ws[j, x + 2] + turned_sum(ws[j, x + 1])
+
+    edge = (lane_full == 0) | (lane_full == Y - 1)
+
     def beside(j, x):
-        v = ws[j, x + 1]
         c = halo[j]
         turned = jnp.concatenate(
             [
@@ -132,10 +142,7 @@
             ],
             axis=0,
         )
-        left = jnp.where(lane_full == 0, turned, pltpu.roll(v, 1, 1))
-        right = jnp.where(lane_full == Y - 1, turned, pltpu.roll(v, Y - 1, 1))
-        total = ws[j, x] + ws[j, x + 2] + left + right
-        return v, total
+        return ws[j, x + 1], bs[j + 1, x] + jnp.where(edge, turned, 0.0)
 
     def through_m(j, x0, x1, v0, v1):
         w0, w1 = matmul(v0, v1)
@@ -193,26 +200,33 @@
     loads[0].wait()
     loads[X - 1].wait()
     even = through_m(0, 0, X - 1, bs[0, 0], bs[0, X - 1])
+
+    def first(i, acc):
+        x0 = 2 * i + 1
+        for x in (x0, x0 + 1):
+            pltpu.make_async_copy(b_hbm.at[:, x, :], bs.at[0, x], load_sem.at[x]).wait()
+        return acc + through_m(0, x0, x0 + 1, bs[0, x0], bs[0, x0 + 1])
+
+    moments[0] = lax.fori_loop(0, (X - 2) // 2, first, even)
     pl.semaphore_wait(barrier, sx - 1 + sy - 1)
+    sent_y = [y_copies(0)]
+    for copy in sent_y[0]:
+        copy.start()
     sent_x = [x_copies(0)]
     for copy in sent_x[0]:
         copy.start()
-    for x in range(1, X - 1):
-        loads[x].wait()
-
-    def first(i, acc):
-        x0 = 2 * i + 1
-        return acc + through_m(0, x0, x0 + 1, bs[0, x0], bs[0, x0 + 1])
-
-    moments[0] = lax.fori_loop(0, (X - 2) // 2, first, even)
-    sent_y = [y_copies(0)]
-    for copy in sent_y[0]:
-        copy.start()
 
     for j in range(ITERS):
+        def ahead(i, carry):
+            periodic(j, 2 * i + 1)
+            periodic(j, 2 * i + 2)
+            return carry
+
+        lax.fori_loop(0, (X - 2) // 2, ahead, 0)
         for copy in sent_y[j]:
             copy.wait()
-        from_left, from_right = pack[ITERS + j], pack[2 * ITERS + j]
+        mine = pack[j]
+        from_left, from_right = pack[ITERS + j] - mine, pack[2 * ITERS + j] - mine
         halo[j] = jnp.where(
             lane % 2 == 0, pltpu.roll(from_left, 1, 1), pltpu.roll(from_right, Y - 1, 1)
         )
@@ -228,15 +242,17 @@
         got = lax.fori_loop(0, (X - 2) // 2, inside, start)
         for copy in sent_x[j]:
             copy.wait()
+        periodic(j, 0)
+        periodic(j, X - 1)
         odd, even = level(j, 0, X - 1)
         moments[2 * j + 1] = got[0] + odd
         if j + 1 < ITERS:
             moments[2 * j + 2] = got[1] + even
+            sent_y.append(y_copies(j + 1))
+            for copy in sent_y[j + 1]:
+                copy.start()
             sent_x.append(x_copies(j + 1))
             for copy in sent_x[j + 1]:
-                copy.start()
-            sent_y.append(y_copies(j + 1))
-            for copy in sent_y[j + 1]:
                 copy.start()
 
     part[...] = jnp.concatenate(
@@ -267,37 +283,48 @@
     summed = jnp.broadcast_to(jnp.sum(total, axis=1, keepdims=True), (8, Y))
     press, resid = coefficients([summed[i:i + 1] for i in range(2 * ITERS)])
 
+    coef[...] = jnp.concatenate(press + resid + [jnp.zeros((1, Y), F32)], axis=0)
+
+
+def combine(bs, ws, coef, p_hbm, r_hbm, p_buf, r_buf, sem):
+    K, X, Y = p_hbm.shape
+    c = [coef[i:i + 1] for i in range(2 * ITERS + 1)]
+    copies = []
     for x in range(X):
-        p = press[0] * ws[0, x + 1]
-        r = resid[0] * bs[0, x]
+        p = c[0] * ws[0, x + 1]
+        r = c[ITERS] * bs[0, x]
         for j in range(1, ITERS):
-            p = p + press[j] * ws[j, x + 1]
+            p = p + c[j] * ws[j, x + 1]
         for j in range(1, ITERS + 1):
-            r = r + resid[j] * bs[j, x]
-        ws[0, x + 1] = p
-        bs[0, x] = r
-        pltpu.make_async_copy(ws.at[0, x + 1], p_hbm.at[:, x, :], store_sem.at[0, x]).start()
-        pltpu.make_async_copy(bs.at[0, x], r_hbm.at[:, x, :], store_sem.at[1, x]).start()
-    for x in range(X):
-        pltpu.make_async_copy(ws.at[0, x + 1], p_hbm.at[:, x, :], store_sem.at[0, x]).wait()
-        pltpu.make_async_copy(bs.at[0, x], r_hbm.at[:, x, :], store_sem.at[1, x]).wait()
+            r = r + c[ITERS + j] * bs[j, x]
+        p_buf[x] = p
+        r_buf[x] = r
+        copies.append(pltpu.make_async_copy(p_buf.at[x], p_hbm.at[:, x, :], sem.at[0, x]))
+        copies.append(pltpu.make_async_copy(r_buf.at[x], r_hbm.at[:, x, :], sem.at[1, x]))
+        copies[-2].start()
+        copies[-1].start()
+    for copy in copies:
+        copy.wait()
 
 
 def on_device(sx, sy, source_heat, horiz_coef, face_coef, column_inverse):
     K, X, Y = source_heat.shape
     KG = K // (Y // (2 * X))
-    any_spec = pl.BlockSpec(memory_space=pl.ANY)
+    hbm = pl.BlockSpec(memory_space=pltpu.HBM)
     vmem = pl.BlockSpec(memory_space=pltpu.VMEM)
     dma = pltpu.SemaphoreType.DMA
-    out = jax.ShapeDtypeStruct((K, X, Y), F32)
-    return pl.pallas_call(
+    bs, ws, coef = pl.pallas_call(
         functools.partial(kernel, sx, sy),
-        out_shape=(out, out),
-        in_specs=[any_spec, vmem, vmem],
-        out_specs=(any_spec, any_spec),
+        out_shape=(
+            jax.ShapeDtypeStruct((ITERS + 1, X, K, Y), F32),
+            jax.ShapeDtypeStruct((ITERS, X + 2, K, Y), F32),
+            jax.ShapeDtypeStruct((8, Y), F32),
+        ),
+        in_specs=[hbm, hbm, hbm],
+        out_specs=(vmem, vmem, vmem),
         scratch_shapes=[
-            pltpu.VMEM((ITERS + 1, X, K, Y), F32),
-            pltpu.VMEM((ITERS, X + 2, K, Y), F32),
+            pltpu.VMEM((1, K), F32),
+            pltpu.VMEM((K, K), F32),
             pltpu.VMEM((K, 3 * K), BF16),
             pltpu.VMEM((3 * ITERS, KG, Y), F32),
             pltpu.VMEM((ITERS, KG, Y), F32),
@@ -306,7 +333,7 @@
             pltpu.VMEM((8, Y), F32),
             pltpu.VMEM((sy - 1, 8, Y), F32),
             dma((X,)),
-            dma((2, X)),
+            dma((2,)),
             dma((ITERS, 2)),
             dma((ITERS, 2)),
             dma((ITERS, 2)),
@@ -317,10 +344,28 @@
             dma((sy - 1,)),
         ],
         compiler_params=pltpu.CompilerParams(
-            collective_id=0, has_side_effects=True, vmem_limit_bytes=40 << 20
+            collective_id=0, has_side_effects=True, vmem_limit_bytes=24 << 20
         ),
         name="pcg",
-    )(source_heat, horiz_coef.reshape(1, K), column_inverse)
+    )(
+        pltpu.with_memory_space_constraint(source_heat, pltpu.HBM),
+        pltpu.with_memory_space_constraint(horiz_coef.reshape(1, K), pltpu.HBM),
+        pltpu.with_memory_space_constraint(column_inverse, pltpu.HBM),
+    )
+    out = jax.ShapeDtypeStruct((K, X, Y), F32)
+    return pl.pallas_call(
+        combine,
+        out_shape=(out, out),
+        in_specs=[vmem, vmem, vmem],
+        out_specs=(hbm, hbm),
+        scratch_shapes=[
+            pltpu.VMEM((X, K, Y), F32),
+            pltpu.VMEM((X, K, Y), F32),
+            dma((2, X)),
+        ],
+        compiler_params=pltpu.CompilerParams(vmem_limit_bytes=24 << 20),
+        name="combine",
+    )(bs, ws, coef)
 
 
 def solution(mesh):

time: 41.7 us -> 35.1 us (0.84)
  local copies, waits for them, and re-layouts: 5.02 us -> 0 us
  Pallas kernels: 35.8 us -> 34.4 us
    unnamed x8 -> x0, local copies, waits for them, and re-layouts: 5.02 us -> none
    pallas_call x1 -> x2, Pallas kernels: 35.8 us -> 34.4 us  [the longest x1 32.6 us: on_device(): pl.pallas_call(functools.partial(kernel, sx, sy), out_shape=(jax.ShapeDty...]
where the time goes in v2:
time: 35.1 us; the launch traced here: 35 us
  Pallas kernels  34.4 us (98%)
  between operations  0.64 us (2%)
    pallas_call x1, Pallas kernels, on_device(): pl.pallas_call(functools.partial(kernel, sx, sy), out_shape=(jax.ShapeDty...  32.6 us
    pallas_call x1, Pallas kernels, on_device(): pl.pallas_call(combine, out_shape=(out, out), in_specs=[vmem, vmem, vmem]...  1.78 us

profile of v2, /device:TPU:0, one launch (start us, length us, event | category | flops | bytes accessed | tf_op | source)
XLA Modules:
  0.0 35.0 jit_solution(13061019794078070583)
XLA Ops:
  0.6 32.6 %pcg.1 = (f32[4,16,160,128]{3,2,1,0:T(8,128)S(1)}, f32[3,18,160,128]{3,2,1,0:T(8,128)S(1)}, f32[8,128]{1,0:T(8,128)S(1)}) custom-call(f32[160,16,128]{2,1,0:T(8,128)} %b_hbm.1, f32[1,160]{1,0:T(1,128)} %bitcast.1, f32[160,160]{1,0:T(8,128)} %m_hbm.1), custom_call_target="tpu_custom_call" | custom-call | tf_op jit(solution)/shard_map/pcg/pallas_call | solution.py:316
  33.2 1.8 %combine.1 = (f32[160,16,128]{2,1,0:T(8,128)}, f32[160,16,128]{2,1,0:T(8,128)}) custom-call(f32[4,16,160,128]{3,2,1,0:T(8,128)S(1)} %get-tuple-element.5.bs, f32[3,18,160,128]{3,2,1,0:T(8,128)S(1)} %get-tuple-element.6.ws, f32[8,128]{1,0:T(8,128)S(1)} %get-tuple-element.7.coef), custom_call_target="tpu_custom_call" | custom-call | tf_op jit(solution)/shard_map/combine/pallas_call | solution.py:356

commit v3 on v2

--- a/solution.py
+++ b/solution.py
@@ -63,9 +63,9 @@
 
 def kernel(
     sx, sy, b_hbm, h_hbm, m_hbm, bs, ws, coef,
-    h_ref, m_ref, mcat, pack, halo, part, slots_x, mid, slots_y,
+    h_ref, m_ref, mcat, pack, halo, part, slots,
     load_sem, small_sem, xs_sem, xr_sem, ys_sem, yr_sem,
-    ax_s, ax_r, ay_s, ay_r,
+    all_s, all_r,
 ):
     K, X, Y = b_hbm.shape
     G = Y // (2 * X)
@@ -75,14 +75,12 @@
     yn, yp = lax.rem(iy + 1, sy), lax.rem(iy + sy - 1, sy)
 
     barrier = pltpu.get_barrier_semaphore()
-    for d in range(1, sx):
-        pl.semaphore_signal(
-            barrier, inc=1, device_id={"gx": lax.rem(ix + d, sx)}, device_id_type=MESH
-        )
-    for d in range(1, sy):
-        pl.semaphore_signal(
-            barrier, inc=1, device_id={"gy": lax.rem(iy + d, sy)}, device_id_type=MESH
-        )
+    peers = [
+        (lax.rem(ix + dx, sx), lax.rem(iy + dy, sy))
+        for dx in range(sx) for dy in range(sy) if dx or dy
+    ]
+    for peer in peers:
+        pl.semaphore_signal(barrier, inc=1, device_id=peer, device_id_type=MESH)
 
     order = [0, X - 1] + list(range(1, X - 1))
     loads = {
@@ -207,8 +205,8 @@
             pltpu.make_async_copy(b_hbm.at[:, x, :], bs.at[0, x], load_sem.at[x]).wait()
         return acc + through_m(0, x0, x0 + 1, bs[0, x0], bs[0, x0 + 1])
 
-    moments[0] = lax.fori_loop(0, (X - 2) // 2, first, even)
-    pl.semaphore_wait(barrier, sx - 1 + sy - 1)
+    moments[0] = lax.fori_loop(0, (X - 2) // 2, first, even, unroll=True)
+    pl.semaphore_wait(barrier, sx * sy - 1)
     sent_y = [y_copies(0)]
     for copy in sent_y[0]:
         copy.start()
@@ -216,13 +214,7 @@
     for copy in sent_x[0]:
         copy.start()
 
-    for j in range(ITERS):
-        def ahead(i, carry):
-            periodic(j, 2 * i + 1)
-            periodic(j, 2 * i + 2)
-            return carry
-
-        lax.fori_loop(0, (X - 2) // 2, ahead, 0)
+    def finish_halo(j):
         for copy in sent_y[j]:
             copy.wait()
         mine = pack[j]
@@ -231,58 +223,91 @@
             lane % 2 == 0, pltpu.roll(from_left, 1, 1), pltpu.roll(from_right, Y - 1, 1)
         )
 
+    pairs = (X - 2) // 2
+    last = ITERS - 1
+    for j in range(last):
+        def ahead(i, carry):
+            periodic(j, 2 * i + 1)
+            periodic(j, 2 * i + 2)
+            return carry
+
+        lax.fori_loop(0, pairs, ahead, 0, unroll=True)
+        finish_halo(j)
+
         def inside(i, acc):
             x0 = 2 * i + 1
             odd, even = level(j, x0, x0 + 1)
-            if even is None:
-                return (acc[0] + odd,)
             return (acc[0] + odd, acc[1] + even)
 
-        start = (zero,) if j + 1 == ITERS else (zero, zero)
-        got = lax.fori_loop(0, (X - 2) // 2, inside, start)
+        got = lax.fori_loop(0, pairs, inside, (zero, zero), unroll=True)
         for copy in sent_x[j]:
             copy.wait()
         periodic(j, 0)
         periodic(j, X - 1)
         odd, even = level(j, 0, X - 1)
         moments[2 * j + 1] = got[0] + odd
-        if j + 1 < ITERS:
-            moments[2 * j + 2] = got[1] + even
-            sent_y.append(y_copies(j + 1))
-            for copy in sent_y[j + 1]:
-                copy.start()
-            sent_x.append(x_copies(j + 1))
-            for copy in sent_x[j + 1]:
-                copy.start()
-
-    part[...] = jnp.concatenate(
+        moments[2 * j + 2] = got[1] + even
+        sent_y.append(y_copies(j + 1))
+        for copy in sent_y[j + 1]:
+            copy.start()
+        sent_x.append(x_copies(j + 1))
+        for copy in sent_x[j + 1]:
+            copy.start()
+
+    def last_row(x):
+        v = ws[last, x + 1]
+        total = ws[last, x] + ws[last, x + 2] + turned_sum(v)
+        bs[last + 1, x] = total
+        return folded(h_b * total * v)
+
+    def last_ahead(i, acc):
+        return acc + last_row(2 * i + 1) + last_row(2 * i + 2)
+
+    odd = lax.fori_loop(0, pairs, last_ahead, zero, unroll=True)
+    group = lax.rem(lane + 1, Y) // (2 * X)
+    h_packed = h_b[:KG]
+    for g in range(1, G):
+        h_packed = jnp.where(group == g, h_b[g * KG:(g + 1) * KG], h_packed)
+    for copy in sent_x[last]:
+        copy.wait()
+    odd = odd + last_row(0) + last_row(X - 1)
+    finish_halo(last)
+    moments[2 * last + 1] = odd + folded(pack[last] * halo[last] * h_packed)
+
+    eight = (8, Y)
+    diagonal = lax.broadcasted_iota(jnp.int32, eight, 0) == lax.broadcasted_iota(
+        jnp.int32, eight, 1
+    )
+    sums = jnp.concatenate(
         [jnp.sum(t, axis=0, keepdims=True) for t in moments]
         + [jnp.zeros((8 - 2 * ITERS, Y), F32)],
         axis=0,
     )
-
-    def total_over(axis, me, size, source, slots, send_sem, recv_sem):
-        copies = []
-        for d in range(1, size):
-            copies.append(
-                pltpu.make_async_remote_copy(
-                    src_ref=source, dst_ref=slots.at[d - 1],
-                    send_sem=send_sem.at[d - 1], recv_sem=recv_sem.at[d - 1],
-                    device_id={axis: lax.rem(me + d, size)}, device_id_type=MESH,
-                )
-            )
-            copies[-1].start()
-        total = source[...]
-        for d in range(1, size):
-            copies[d - 1].wait()
-            total = total + slots[d - 1]
-        return total
-
-    mid[...] = total_over("gx", ix, sx, part, slots_x, ax_s, ax_r)
-    total = total_over("gy", iy, sy, mid, slots_y, ay_s, ay_r)
-    summed = jnp.broadcast_to(jnp.sum(total, axis=1, keepdims=True), (8, Y))
+    sums = jnp.sum(sums, axis=1, keepdims=True)
+    part[...] = jnp.sum(jnp.where(diagonal, sums, 0.0), axis=0, keepdims=True)
+    copies = [
+        pltpu.make_async_remote_copy(
+            src_ref=part, dst_ref=slots.at[d],
+            send_sem=all_s.at[d], recv_sem=all_r.at[d],
+            device_id=peer, device_id_type=MESH,
+        )
+        for d, peer in enumerate(peers)
+    ]
+    for copy in copies:
+        copy.start()
+
+    def corrected(i, carry):
+        for x in (2 * i, 2 * i + 1):
+            bs[last + 1, x] = h_b * beside(last, x)[1]
+        return carry
+
+    lax.fori_loop(0, X // 2, corrected, 0, unroll=True)
+    for copy in copies:
+        copy.wait()
+    total = part[...] + jnp.sum(slots[...], axis=0)
+    summed = jnp.sum(jnp.where(diagonal, total, 0.0), axis=1, keepdims=True)
+    summed = jnp.broadcast_to(summed, eight)
     press, resid = coefficients([summed[i:i + 1] for i in range(2 * ITERS)])
-
     coef[...] = jnp.concatenate(press + resid + [jnp.zeros((1, Y), F32)], axis=0)
 
 
@@ -328,20 +353,16 @@
             pltpu.VMEM((K, 3 * K), BF16),
             pltpu.VMEM((3 * ITERS, KG, Y), F32),
             pltpu.VMEM((ITERS, KG, Y), F32),
-            pltpu.VMEM((8, Y), F32),
-            pltpu.VMEM((sx - 1, 8, Y), F32),
-            pltpu.VMEM((8, Y), F32),
-            pltpu.VMEM((sy - 1, 8, Y), F32),
+            pltpu.VMEM((1, Y), F32),
+            pltpu.VMEM((sx * sy - 1, 1, Y), F32),
             dma((X,)),
             dma((2,)),
             dma((ITERS, 2)),
             dma((ITERS, 2)),
             dma((ITERS, 2)),
             dma((ITERS, 2)),
-            dma((sx - 1,)),
-            dma((sx - 1,)),
-            dma((sy - 1,)),
-            dma((sy - 1,)),
+            dma((sx * sy - 1,)),
+            dma((sx * sy - 1,)),
         ],
         compiler_params=pltpu.CompilerParams(
             collective_id=0, has_side_effects=True, vmem_limit_bytes=24 << 20

time: 35.1 us -> 32.7 us (0.932)
  Pallas kernels: 34.4 us -> 31.9 us
    pallas_call x1, Pallas kernels: 32.6 us -> 30.2 us  [on_device(): pl.pallas_call(functools.partial(kernel, sx, sy), out_shape=(jax.ShapeDty...]
where the time goes in v3:
time: 32.7 us; the launch traced here: 32.6 us
  Pallas kernels  31.9 us (98%)
  between operations  0.64 us (2%)
    pallas_call x1, Pallas kernels, on_device(): pl.pallas_call(functools.partial(kernel, sx, sy), out_shape=(jax.ShapeDty...  30.2 us
    pallas_call x1, Pallas kernels, on_device(): pl.pallas_call(combine, out_shape=(out, out), in_specs=[vmem, vmem, vmem]...  1.78 us

profile of v3, /device:TPU:0, one launch (start us, length us, event | category | flops | bytes accessed | tf_op | source)
XLA Modules:
  0.0 32.6 jit_solution(15598892488061903124)
XLA Ops:
  0.6 30.2 %pcg.1 = (f32[4,16,160,128]{3,2,1,0:T(8,128)S(1)}, f32[3,18,160,128]{3,2,1,0:T(8,128)S(1)}, f32[8,128]{1,0:T(8,128)S(1)}) custom-call(f32[160,16,128]{2,1,0:T(8,128)} %b_hbm.1, f32[1,160]{1,0:T(1,128)} %bitcast.1, f32[160,160]{1,0:T(8,128)} %m_hbm.1), custom_call_target="tpu_custom_call" | custom-call | tf_op jit(solution)/shard_map/pcg/pallas_call | solution.py:341
  30.8 1.8 %combine.1 = (f32[160,16,128]{2,1,0:T(8,128)}, f32[160,16,128]{2,1,0:T(8,128)}) custom-call(f32[4,16,160,128]{3,2,1,0:T(8,128)S(1)} %get-tuple-element.5.bs, f32[3,18,160,128]{3,2,1,0:T(8,128)S(1)} %get-tuple-element.6.ws, f32[8,128]{1,0:T(8,128)S(1)} %get-tuple-element.7.coef), custom_call_target="tpu_custom_call" | custom-call | tf_op jit(solution)/shard_map/combine/pallas_call | solution.py:377

commit v4 on v3

--- a/solution.py
+++ b/solution.py
@@ -63,7 +63,7 @@
 
 def kernel(
     sx, sy, b_hbm, h_hbm, m_hbm, bs, ws, coef,
-    h_ref, m_ref, mcat, pack, halo, part, slots,
+    h_ref, m_ref, mcat, pack, halo, h_full, part, slots,
     load_sem, small_sem, xs_sem, xr_sem, ys_sem, yr_sem,
     all_s, all_r,
 ):
@@ -101,7 +101,7 @@
     rows = lax.broadcasted_iota(jnp.int32, (K, K), 0)
     cols = lax.broadcasted_iota(jnp.int32, (K, K), 1)
     h_col = jnp.sum(jnp.where(rows == cols, h_ref[...], 0.0), axis=1, keepdims=True)
-    h_b = jnp.broadcast_to(h_col, (K, Y))
+    h_full[...] = jnp.broadcast_to(h_col, (K, Y))
     lane = lax.broadcasted_iota(jnp.int32, (KG, Y), 1)
     lane_full = lax.broadcasted_iota(jnp.int32, (K, Y), 1)
 
@@ -127,7 +127,15 @@
         return pltpu.roll(v, 1, 1) + pltpu.roll(v, Y - 1, 1)
 
     def periodic(j, x):
-        bs[j + 1, x] = ws[j, x] + ws[j, x + 2] + turned_sum(ws[j, x + 1])
+        v = ws[j, x + 1]
+        total = ws[j, x] + ws[j, x + 2] + turned_sum(v)
+        bs[j + 1, x] = total
+        return folded(bs[j, x] * v), folded(h_full[...] * total * v)
+
+    def periodic_two(j, x0, x1, acc):
+        even0, odd0 = periodic(j, x0)
+        even1, odd1 = periodic(j, x1)
+        return acc[0] + (even0 + even1), acc[1] + (odd0 + odd1)
 
     edge = (lane_full == 0) | (lane_full == Y - 1)
 
@@ -148,19 +156,14 @@
         ws[j, x1 + 1] = w1
         packed(j, x0, w0)
         packed(j, x1, w1)
-        return folded(v0 * w0 + v1 * w1)
 
     def level(j, x0, x1):
         w0, s0 = beside(j, x0)
         w1, s1 = beside(j, x1)
-        b0, b1 = h_b * s0, h_b * s1
+        b0, b1 = h_full[...] * s0, h_full[...] * s1
         bs[j + 1, x0] = b0
         bs[j + 1, x1] = b1
-        odd = folded(b0 * w0 + b1 * w1)
-        even = None
-        if j + 1 < ITERS:
-            even = through_m(j + 1, x0, x1, b0, b1)
-        return odd, even
+        through_m(j + 1, x0, x1, b0, b1)
 
     def x_copies(j):
         return (
@@ -197,15 +200,16 @@
 
     loads[0].wait()
     loads[X - 1].wait()
-    even = through_m(0, 0, X - 1, bs[0, 0], bs[0, X - 1])
+    through_m(0, 0, X - 1, bs[0, 0], bs[0, X - 1])
 
     def first(i, acc):
         x0 = 2 * i + 1
         for x in (x0, x0 + 1):
             pltpu.make_async_copy(b_hbm.at[:, x, :], bs.at[0, x], load_sem.at[x]).wait()
-        return acc + through_m(0, x0, x0 + 1, bs[0, x0], bs[0, x0 + 1])
-
-    moments[0] = lax.fori_loop(0, (X - 2) // 2, first, even, unroll=True)
+        through_m(0, x0, x0 + 1, bs[0, x0], bs[0, x0 + 1])
+        return acc
+
+    lax.fori_loop(0, (X - 2) // 2, first, 0, unroll=True)
     pl.semaphore_wait(barrier, sx * sy - 1)
     sent_y = [y_copies(0)]
     for copy in sent_y[0]:
@@ -225,54 +229,38 @@
 
     pairs = (X - 2) // 2
     last = ITERS - 1
-    for j in range(last):
-        def ahead(i, carry):
-            periodic(j, 2 * i + 1)
-            periodic(j, 2 * i + 2)
-            return carry
-
-        lax.fori_loop(0, pairs, ahead, 0, unroll=True)
+    group = lax.rem(lane + 1, Y) // (2 * X)
+    h_packed = h_full[:KG]
+    for g in range(1, G):
+        h_packed = jnp.where(group == g, h_full[g * KG:(g + 1) * KG], h_packed)
+    for j in range(ITERS):
+        def ahead(i, acc):
+            return periodic_two(j, 2 * i + 1, 2 * i + 2, acc)
+
+        got = lax.fori_loop(0, pairs, ahead, (zero, zero), unroll=True)
+        if j == last:
+            for copy in sent_x[j]:
+                copy.wait()
+            got = periodic_two(j, 0, X - 1, got)
         finish_halo(j)
-
-        def inside(i, acc):
-            x0 = 2 * i + 1
-            odd, even = level(j, x0, x0 + 1)
-            return (acc[0] + odd, acc[1] + even)
-
-        got = lax.fori_loop(0, pairs, inside, (zero, zero), unroll=True)
-        for copy in sent_x[j]:
-            copy.wait()
-        periodic(j, 0)
-        periodic(j, X - 1)
-        odd, even = level(j, 0, X - 1)
-        moments[2 * j + 1] = got[0] + odd
-        moments[2 * j + 2] = got[1] + even
-        sent_y.append(y_copies(j + 1))
-        for copy in sent_y[j + 1]:
-            copy.start()
-        sent_x.append(x_copies(j + 1))
-        for copy in sent_x[j + 1]:
-            copy.start()
-
-    def last_row(x):
-        v = ws[last, x + 1]
-        total = ws[last, x] + ws[last, x + 2] + turned_sum(v)
-        bs[last + 1, x] = total
-        return folded(h_b * total * v)
-
-    def last_ahead(i, acc):
-        return acc + last_row(2 * i + 1) + last_row(2 * i + 2)
-
-    odd = lax.fori_loop(0, pairs, last_ahead, zero, unroll=True)
-    group = lax.rem(lane + 1, Y) // (2 * X)
-    h_packed = h_b[:KG]
-    for g in range(1, G):
-        h_packed = jnp.where(group == g, h_b[g * KG:(g + 1) * KG], h_packed)
-    for copy in sent_x[last]:
-        copy.wait()
-    odd = odd + last_row(0) + last_row(X - 1)
-    finish_halo(last)
-    moments[2 * last + 1] = odd + folded(pack[last] * halo[last] * h_packed)
+        if j < last:
+            def inside(i, carry):
+                level(j, 2 * i + 1, 2 * i + 2)
+                return carry
+
+            lax.fori_loop(0, pairs, inside, 0, unroll=True)
+            for copy in sent_x[j]:
+                copy.wait()
+            got = periodic_two(j, 0, X - 1, got)
+            level(j, 0, X - 1)
+            sent_y.append(y_copies(j + 1))
+            for copy in sent_y[j + 1]:
+                copy.start()
+            sent_x.append(x_copies(j + 1))
+            for copy in sent_x[j + 1]:
+                copy.start()
+        moments[2 * j] = got[0]
+        moments[2 * j + 1] = got[1] + folded(pack[j] * halo[j] * h_packed)
 
     eight = (8, Y)
     diagonal = lax.broadcasted_iota(jnp.int32, eight, 0) == lax.broadcasted_iota(
@@ -298,7 +286,7 @@
 
     def corrected(i, carry):
         for x in (2 * i, 2 * i + 1):
-            bs[last + 1, x] = h_b * beside(last, x)[1]
+            bs[last + 1, x] = h_full[...] * beside(last, x)[1]
         return carry
 
     lax.fori_loop(0, X // 2, corrected, 0, unroll=True)
@@ -353,6 +341,7 @@
             pltpu.VMEM((K, 3 * K), BF16),
             pltpu.VMEM((3 * ITERS, KG, Y), F32),
             pltpu.VMEM((ITERS, KG, Y), F32),
+            pltpu.VMEM((K, Y), F32),
             pltpu.VMEM((1, Y), F32),
             pltpu.VMEM((sx * sy - 1, 1, Y), F32),
             dma((X,)),

time: 32.7 us -> 32.7 us (level)
  no operation moved by 1% of the time
where the time goes in v4:
time: 32.7 us; the launch traced here: 32.6 us
  Pallas kernels  31.9 us (98%)
  between operations  0.64 us (2%)
    pallas_call x1, Pallas kernels, on_device(): pl.pallas_call(functools.partial(kernel, sx, sy), out_shape=(jax.ShapeDty...  30.2 us
    pallas_call x1, Pallas kernels, on_device(): pl.pallas_call(combine, out_shape=(out, out), in_specs=[vmem, vmem, vmem]...  1.78 us

profile of v4, /device:TPU:0, one launch (start us, length us, event | category | flops | bytes accessed | tf_op | source)
XLA Modules:
  0.0 32.6 jit_solution(7530390114949224759)
XLA Ops:
  0.6 30.2 %pcg.1 = (f32[4,16,160,128]{3,2,1,0:T(8,128)S(1)}, f32[3,18,160,128]{3,2,1,0:T(8,128)S(1)}, f32[8,128]{1,0:T(8,128)S(1)}) custom-call(f32[160,16,128]{2,1,0:T(8,128)} %b_hbm.1, f32[1,160]{1,0:T(1,128)} %bitcast.1, f32[160,160]{1,0:T(8,128)} %m_hbm.1), custom_call_target="tpu_custom_call" | custom-call | tf_op jit(solution)/shard_map/pcg/pallas_call | solution.py:329
  30.8 1.8 %combine.1 = (f32[160,16,128]{2,1,0:T(8,128)}, f32[160,16,128]{2,1,0:T(8,128)}) custom-call(f32[4,16,160,128]{3,2,1,0:T(8,128)S(1)} %get-tuple-element.5.bs, f32[3,18,160,128]{3,2,1,0:T(8,128)S(1)} %get-tuple-element.6.ws, f32[8,128]{1,0:T(8,128)S(1)} %get-tuple-element.7.coef), custom_call_target="tpu_custom_call" | custom-call | tf_op jit(solution)/shard_map/combine/pallas_call | solution.py:366
